TPU v7x, 512 devices: a whole 4x4x16 slice. The times are simulated.
512 devices in a mesh: slab: 64 (over z, y), mem: 8 (over x, core).
Axes of the slice: x: 4, y: 4, z: 16, core: 2. Of those that a mesh axis runs over, the one named last changes fastest.
Arguments:
- present_ensemble: float32 [64, 4, 64, 512], P('mem', None, 'slab'), may hold values from -6 to 6
- delayed_ensemble: float32 [64, 2, 4, 64, 512], P('mem', None, None, 'slab'), may hold values from -6 to 6
- spreading_coefficient: float32 [64, 512], P('slab'), may hold values from 0.05 to 0.2
- transport_ratios: float32 [2, 64, 512], P(None, 'slab'), may hold values from -0.3 to 0.3
- obs_value: float32 [2, 256], replicated, may hold values from -6 to 6
- obs_error: float32 [2, 256], replicated, may hold values from 0.4 to 1.2
- obs_noise: float32 [2, 64, 256], replicated, may hold values from -6 to 6
- obs_row: int32 [2, 256], replicated, may hold values from 0 to 63
- obs_col: int32 [2, 256], replicated, may hold values from 1 to 510
- obs_field: int32 [2, 256], replicated, may hold values from 0 to 3
Outputs:
- analysis: float32 [64, 3, 4, 64, 512], P('mem', None, None, 'slab')
All inputs are finite; a program needn't handle non-finite values.
Results may differ from a plain program's by a relative error of at most 0.00011.
Values sent between devices are 32-bit elements; how exact they have to be, the bound alone decides.
A program may use at most 64 MiB of HBM per device.

v0:
```python
import jax
import jax.numpy as jnp
from jax import lax
from jax.sharding import PartitionSpec as P


def extended(shard, sides, width):
    for axis, dim in sides:
        devices, length = (lax.axis_size(axis), shard.shape[dim])
        up = [(i, (i + 1) % devices) for i in range(devices - 1)]
        down = [(j, i) for i, j in up]
        last = lax.slice_in_dim(shard, length - width, length, axis=dim)
        leading = lax.slice_in_dim(shard, 0, width, axis=dim)
        before = lax.ppermute(last, axis, up)
        after = lax.ppermute(leading, axis, down)
        shard = jnp.concatenate([before, shard, after], axis=dim)
    return shard


def propagate_ahead(present_ensemble, spreading_coefficient, transport_ratios):
    rowed = extended(present_ensemble, (("slab", 2),), 1)
    padded = jnp.pad(rowed, ((0, 0), (0, 0), (0, 0), (1, 1)))
    below = padded[:, :, 2:, 1:-1]
    above = padded[:, :, :-2, 1:-1]
    right = padded[:, :, 1:-1, 2:]
    left = padded[:, :, 1:-1, :-2]
    laplacian_operator = below + above + right + left - 4.0 * present_ensemble
    return (
        present_ensemble
        + spreading_coefficient * laplacian_operator
        - transport_ratios[0] * (below - above) * 0.5
        - transport_ratios[1] * (right - left) * 0.5
    )


def observe(level_zero, rows, cols, fields, row_start, col_start):
    members, nfield, height, width = level_zero.shape
    flat = level_zero.reshape(members, nfield * height * width)
    total = jnp.zeros((members, rows.shape[0]), jnp.float32)
    for offset, factor in ((-1, 0.25), (0, 0.5), (1, 0.25)):
        row_within = rows - row_start
        column_within = cols + offset - col_start
        valid = (
            (row_within >= 0)
            & (row_within < height)
            & (column_within >= 0)
            & (column_within < width)
        )
        index = (fields * height + jnp.clip(row_within, 0, height - 1)) * width + jnp.clip(
            column_within, 0, width - 1
        )
        picked = jnp.take(flat, index, axis=1)
        total = total + factor * jnp.where(valid[None, :], picked, 0.0)
    return total


def transform(observed, values, errors, noise):
    members = observed.shape[0]
    rescaled_values = (observed - jnp.mean(observed, axis=0, keepdims=True)) / errors[None, :]
    innovation = (values[None, :] - observed) / errors[None, :] + noise
    eye = jnp.eye(members, dtype=jnp.float32)
    system = (
        jnp.dot(
            rescaled_values,
            rescaled_values.T,
            precision=lax.Precision.HIGHEST,
            preferred_element_type=jnp.float32,
        )
        + (members - 1.0) * eye
    )
    right = jnp.dot(
        rescaled_values,
        innovation.T,
        precision=lax.Precision.HIGHEST,
        preferred_element_type=jnp.float32,
    )
    factor = jnp.linalg.cholesky(system)
    middle = lax.linalg.triangular_solve(factor, right, left_side=True, lower=True)
    weights = lax.linalg.triangular_solve(
        factor, middle, left_side=True, lower=True, transpose_a=True
    )
    return eye + weights - jnp.mean(weights, axis=0, keepdims=True)


def shards(
    present_ensemble,
    delayed_ensemble,
    spreading_coefficient,
    transport_ratios,
    obs_value,
    obs_error,
    obs_noise,
    obs_row,
    obs_col,
    obs_field,
):
    rows_here = present_ensemble.shape[2]
    row_start = lax.axis_index("slab") * rows_here
    predictive_dynamics = propagate_ahead(present_ensemble, spreading_coefficient, transport_ratios)
    flattened_system_array = jnp.concatenate(
        [predictive_dynamics[:, None], delayed_ensemble], axis=1
    )
    batch_count = obs_row.shape[0]
    columns = lax.all_to_all(flattened_system_array, "mem", split_axis=4, concat_axis=0, tiled=True)
    col_start = lax.axis_index("mem") * columns.shape[4]
    for batch in range(batch_count):
        partial_obs = observe(
            columns[:, 0], obs_row[batch], obs_col[batch], obs_field[batch], row_start, col_start
        )
        observed = lax.psum(partial_obs, ("slab", "mem"))
        matrix = transform(observed, obs_value[batch], obs_error[batch], obs_noise[batch])
        columns = jnp.einsum("jlfrn,jm->mlfrn", columns, matrix, precision=lax.Precision.HIGHEST)
    return lax.all_to_all(columns, "mem", split_axis=0, concat_axis=4, tiled=True)


def solution(mesh):
    return jax.shard_map(
        shards,
        mesh=mesh,
        in_specs=(
            P("mem", None, "slab", None),
            P("mem", None, None, "slab", None),
            P("slab", None),
            P(None, "slab", None),
            P(),
            P(),
            P(),
            P(),
            P(),
            P(),
        ),
        out_specs=P("mem", None, None, "slab", None),
        check_vma=False,
    )
```

profile of v0, /device:TPU:1, one launch (start us, length us, event | category | flops | bytes accessed | tf_op | source)
XLA Modules:
  0.0 1024.7 jit_solution(14442951278854169686)
XLA Ops:
  6.5 0.9 copy.140
  7.5 1.3 collective-permute-start
  8.8 4.7 collective-permute-start.1
  13.4 0.8 clamp_add_fusion.2
  14.2 0.8 clamp_add_fusion.1
  16.2 0.8 compare_and_fusion
  17.6 2.6 copy.142
  20.2 0.7 fusion.52
  20.9 1.5 fusion.51
  23.0 1.3 fusion.54
  24.3 1.3 fusion.53
  26.2 1.4 and_reduce_fusion.5
  27.8 1.3 copy.141
  29.2 2.7 fusion.57
  31.8 4.3 reshape.204
  36.1 10.0 all-to-all-start
  46.8 5.3 all-to-all-done
  52.6 1.0 reduce.16
  53.6 3.7 reshape.205
  57.3 1.5 copy.166
  59.0 0.7 gather_fusion.2
  59.7 0.7 gather_fusion.1
  60.4 0.9 gather_fusion
  61.4 1.6 fusion.11
  63.3 0.6 pad_clamp_fusion.2
  63.9 0.9 copy.170
  64.8 455.5 %all-reduce.4.cloned.1.call-done = f32[64,256]{0,1:T(8,128)} async-done(((f32[64,256]{0,1:T(8,128)}), f32[64,256]{0,1:T(8,128)}) %all-reduce.4.cloned.1.call-update) | async-done | bytes 65552 | tf_op jit(solution)/shard_map/psum | solution.py:110
  520.4 1.0 reduce_sum.36
  521.4 1.5 convolution_add_fusion.1
  523.1 5.8 cholesky.44
  528.9 0.6 compare_reduce_fusion.1
  529.6 0.7 fusion.29
  530.3 4.9 custom-call.11
  535.2 1.5 fusion.9
  537.9 0.7 gather_fusion.5
  538.6 0.7 gather_fusion.4
  539.3 0.7 gather_fusion.3
  540.1 0.9 fusion.5
  541.2 447.2 %all-reduce.6.cloned.1.call-done = f32[64,256]{0,1:T(8,128)} async-done(((f32[64,256]{0,1:T(8,128)}), f32[64,256]{0,1:T(8,128)}) %all-reduce.6.cloned.1.call-update) | async-done | bytes 65552 | tf_op jit(solution)/shard_map/psum | solution.py:110
  988.4 1.0 reduce_sum.38
  989.4 1.5 convolution_add_fusion
  991.1 5.8 cholesky.55
  997.6 0.7 fusion.30
  998.3 4.9 custom-call.13
  1003.2 1.5 fusion.3
  1006.4 9.0 all_to_all.36
  1015.4 1.0 reduce.17
  1017.0 0.9 all_to_all.33
  (78 shorter events, 8.9 us)
Async XLA Ops:
  6.5 21.2 %copy-start = (f32[8,4,1,512]{3,2,1,0:T(1,128)S(1)}, f32[8,4,1,512]{3,2,1,0:T(1,128)}, u32[]{:S(2)}) copy-start(f32[8,4,1,512]{3,2,1,0:T(1,128)} %param.17) | copy-start | bytes 196612
  6.5 21.2 %copy-start.2 = (f32[1,512]{1,0:T(1,128)S(1)}, f32[1,512]{1,0:T(1,128)}, u32[]{:S(2)}) copy-start(f32[1,512]{1,0:T(1,128)} %param.19) | copy-start | bytes 6148
  7.5 20.1 %collective-permute-start = (f32[8,4,1,512]{3,0,2,1:T(8,128)S(1)}, f32[8,4,1,512]{3,0,2,1:T(8,128)S(1)}, u32[]{:S(2)}, u32[]{:S(2)}) collective-permute-start(f32[8,4,1,512]{3,0,2,1:T(8,128)S(1)} %copy.140), channel_id=1, source_target_pairs={{8,0},{16,8},{24,16},{32,24},{40,32},{48,40},{56,48},{64,56},{72,6... | collective-permute-start | bytes 196616 | tf_op jit(solution)/shard_map/ppermute | solution.py:15
  8.8 18.8 %collective-permute-start.1 = (f32[8,4,1,512]{3,0,2,1:T(8,128)S(1)}, f32[8,4,1,512]{3,0,2,1:T(8,128)S(1)}, u32[]{:S(2)}, u32[]{:S(2)}) collective-permute-start(f32[8,4,1,512]{3,0,2,1:T(8,128)S(1)} %copy.140), channel_id=1, source_target_pairs={{0,8},{8,16},{16,24},{24,32},{32,40},{40,48},{48,56},{56,64},{64,7... | collective-permute-start | bytes 196616 | tf_op jit(solution)/shard_map/ppermute | solution.py:14
  36.1 15.9 %all-to-all-start = ((f32[8,1,6144]{2,1,0:T(1,128)}), f32[8,1,6144]{2,1,0:T(1,128)S(1)}, u32[]{:S(2)}, u32[]{:S(2)}) async-start(f32[8,1,6144]{2,1,0:T(1,128)} %reshape.204), calls=%async_computation | async-start | bytes 393216 | tf_op jit(solution)/shard_map/all_to_all | solution.py:104
  46.2 474.2 %all-reduce.4.cloned.1.call-start = ((), (), s32[]{:S(2)}) async-start(), calls=%async_computation.2 | async-start | bytes 262144 | tf_op jit(solution)/shard_map/psum | solution.py:110
  58.9 462.6 %copy-start.11 = (f32[1,256]{1,0:T(1,128)S(1)}, f32[1,256]{1,0:T(1,128)}, u32[]{:S(2)}) copy-start(f32[1,256]{1,0:T(1,128)} %get-tuple-element.33) | copy-start | bytes 3076
  58.9 476.3 %copy-start.10 = (f32[1,256]{1,0:T(1,128)S(1)}, f32[1,256]{1,0:T(1,128)}, u32[]{:S(2)}) copy-start(f32[1,256]{1,0:T(1,128)} %get-tuple-element.35) | copy-start | bytes 3076
  61.3 478.8 %copy-start.3 = (pred[256]{0:T(512)(128)(4,1)S(1)}, pred[256]{0:T(512)(128)(4,1)}, u32[]{:S(2)}) copy-start(pred[256]{0:T(512)(128)(4,1)} %get-tuple-element.46) | copy-start | bytes 772
  61.3 478.8 %copy-start.4 = (pred[256]{0:T(512)(128)(4,1)S(1)}, pred[256]{0:T(512)(128)(4,1)}, u32[]{:S(2)}) copy-start(pred[256]{0:T(512)(128)(4,1)} %get-tuple-element.47) | copy-start | bytes 772
  61.3 478.8 %copy-start.5 = (pred[256]{0:T(512)(128)(4,1)S(1)}, pred[256]{0:T(512)(128)(4,1)}, u32[]{:S(2)}) copy-start(pred[256]{0:T(512)(128)(4,1)} %get-tuple-element.6) | copy-start | bytes 772
  61.3 478.8 %copy-start.6 = (pred[256]{0:T(512)(128)(4,1)S(1)}, pred[256]{0:T(512)(128)(4,1)}, u32[]{:S(2)}) copy-start(pred[256]{0:T(512)(128)(4,1)} %get-tuple-element.8) | copy-start | bytes 772
  61.3 478.8 %copy-start.7 = (pred[256]{0:T(512)(128)(4,1)S(1)}, pred[256]{0:T(512)(128)(4,1)}, u32[]{:S(2)}) copy-start(pred[256]{0:T(512)(128)(4,1)} %get-tuple-element.10) | copy-start | bytes 772
  61.4 478.8 %copy-start.12 = (pred[256]{0:T(512)(128)(4,1)S(1)}, pred[256]{0:T(512)(128)(4,1)}, u32[]{:S(2)}) copy-start(pred[256]{0:T(512)(128)(4,1)} %compare_and_fusion.4) | copy-start | bytes 772
  63.0 478.1 %copy-start.1 = (f32[1,64,256]{2,1,0:T(8,128)S(1)}, f32[1,64,256]{2,1,0:T(8,128)}, u32[]{:S(2)}) copy-start(f32[1,64,256]{2,1,0:T(8,128)} %get-tuple-element.22) | copy-start | bytes 196612
  63.0 925.4 %all-reduce.6.cloned.1.call-start = ((), (), s32[]{:S(2)}) async-start(), calls=%async_computation.3 | async-start | bytes 262144 | tf_op jit(solution)/shard_map/psum | solution.py:110
  521.4 468.0 %copy-start.9 = (f32[1,256]{1,0:T(1,128)S(1)}, f32[1,256]{1,0:T(1,128)}, u32[]{:S(2)}) copy-start(f32[1,256]{1,0:T(1,128)} %get-tuple-element.32) | copy-start | bytes 3076
  530.2 472.9 %copy-start.8 = (f32[1,256]{1,0:T(1,128)S(1)}, f32[1,256]{1,0:T(1,128)}, u32[]{:S(2)}) copy-start(f32[1,256]{1,0:T(1,128)} %get-tuple-element.34) | copy-start | bytes 3076
Sparse Core Ops, SparseCore 0:
  63.1 457.1 all-reduce.3
  541.2 447.1 all-reduce.5
where the time goes:
time: 1030 us; the launch traced here: 1020 us
  waiting for transfers between devices  908 us (88%)
  other arithmetic  41.6 us (4%)
  local copies, waits for them, and re-layouts  27.9 us (3%)
  starting transfers between devices  16.2 us (2%)
  between operations  13.9 us (1%)
    psum x2, waiting for transfers between devices, shards(): observed = lax.psum(partial_obs, ('slab', 'mem'))  903 us
  transfers between devices with their start and end apart: 5, of which 3 were waited for; matrix products, arithmetic and copies ran while one was open for 2% of the time, Pallas kernels for 0%

commit v1 on v0

--- a/solution.py
+++ b/solution.py
@@ -2,6 +2,7 @@
 import jax.numpy as jnp
 from jax import lax
 from jax.sharding import PartitionSpec as P
+from jax.lax import all_gather
 
 
 def extended(shard, sides, width):
@@ -107,7 +108,7 @@
         partial_obs = observe(
             columns[:, 0], obs_row[batch], obs_col[batch], obs_field[batch], row_start, col_start
         )
-        observed = lax.psum(partial_obs, ("slab", "mem"))
+        observed = jnp.sum(all_gather(partial_obs, ("slab", "mem")), axis=0)
         matrix = transform(observed, obs_value[batch], obs_error[batch], obs_noise[batch])
         columns = jnp.einsum("jlfrn,jm->mlfrn", columns, matrix, precision=lax.Precision.HIGHEST)
     return lax.all_to_all(columns, "mem", split_axis=0, concat_axis=4, tiled=True)

time: 1030 us -> 637 us (0.62)
  waiting for transfers between devices: 908 us -> 473 us
  other arithmetic: 41.6 us -> 94.6 us
    psum x2 -> x0, waiting for transfers between devices: 903 us -> none  [shards(): observed = lax.psum(partial_obs, ('slab', 'mem'))]
    all_gather x0 -> x2, waiting for transfers between devices: none -> 468 us  [shards(): observed = jnp.sum(all_gather(partial_obs, ('slab', 'mem')), axis=0)]
    reduce_sum x2, other arithmetic: 2.01 us -> 30 us  [transform(): jnp.mean(observed, axis=0, keepdims=True)]
    reduce_sum x0 -> x2, other arithmetic: none -> 25.9 us  [shards(): observed = jnp.sum(all_gather(partial_obs, ('slab', 'mem')), axis=0)]
where the time goes in v1:
time: 637 us; the launch traced here: 636 us
  waiting for transfers between devices  473 us (74%)
  other arithmetic  94.6 us (15%)
  local copies, waits for them, and re-layouts  24.8 us (4%)
  starting transfers between devices  16.2 us (3%)
  between operations  13.8 us (2%)
  blocking collectives  10.2 us (2%)
    all_gather x2, waiting for transfers between devices, shards(): observed = jnp.sum(all_gather(partial_obs, ('slab', 'mem')), axis=0)  468 us
    reduce_sum x2, other arithmetic, transform(): jnp.mean(observed, axis=0, keepdims=True)  30 us
    reduce_sum x2, other arithmetic, shards(): observed = jnp.sum(all_gather(partial_obs, ('slab', 'mem')), axis=0)  25.9 us
    another operation x6, other arithmetic, transform(): factor = jnp.linalg.cholesky(system)  13 us
  transfers between devices with their start and end apart: 5, of which 3 were waited for; matrix products, arithmetic and copies ran while one was open for 2% of the time, Pallas kernels for 0%

profile of v1, /device:TPU:1, one launch (start us, length us, event | category | flops | bytes accessed | tf_op | source)
XLA Modules:
  0.0 635.5 jit_solution(16074655929105383639)
XLA Ops:
  6.5 0.9 copy.138
  7.4 1.3 collective-permute-start
  8.7 4.7 collective-permute-start.1
  13.4 1.4 clamp_add_fusion.2
  14.7 0.8 clamp_add_fusion.1
  15.5 0.6 compare_and_fusion.5
  16.1 0.8 compare_and_fusion
  16.9 0.7 fusion.53
  17.6 2.6 copy.140
  20.2 1.4 and_reduce_fusion.5
  22.3 1.0 subtract_bitcast_fusion
  23.3 1.3 copy.139
  24.6 2.7 fusion.58
  27.3 4.3 reshape.206
  31.6 10.0 %all-to-all-start = ((f32[8,1,6144]{2,1,0:T(1,128)}), f32[8,1,6144]{2,1,0:T(1,128)S(1)}, u32[]{:S(2)}, u32[]{:S(2)}) async-start(f32[8,1,6144]{2,1,0:T(1,128)} %reshape.206), calls=%async_computation | async-start | bytes 393216 | tf_op jit(solution)/shard_map/all_to_all | solution.py:105
  42.2 5.3 all-to-all-done
  48.0 1.0 reduce.20
  49.0 3.7 reshape.207
  52.8 1.5 copy.164
  54.4 0.7 gather_fusion.1
  55.1 0.7 gather_fusion.2
  55.9 0.9 gather_fusion
  56.7 1.0 fusion.9
  57.7 0.7 copy.144
  58.7 0.7 compare_select_fusion.2
  59.4 0.7 compare_and_fusion.4
  60.1 0.8 fusion.54
  60.9 235.9 %all-gather.5.cloned.1.call-done = f32[32768,256]{1,0:T(8,128)} async-done(((f32[64,256]{1,0:T(8,128)}), f32[32768,256]{1,0:T(8,128)}) %all-gather.5.cloned.1.call-update) | async-done | bytes 33554448 | tf_op jit(solution)/shard_map/all_gather | solution.py:111
  296.8 12.9 %reduce_sum.54 = f32[64,256]{1,0:T(8,128)S(1)} reduce(f32[512,64,256]{2,1,0:T(8,128)} %bitcast.137, f32[]{:T(128)} %constant.76.clone.1), dimensions={0}, to_apply=%region_0.2 | reduce | flops 8372224 | bytes 33619972 | tf_op jit(solution)/shard_map/reduce_sum | solution.py:111
  309.7 15.0 %reduce_sum.55 = f32[256]{0:T(256)S(1)} reduce(f32[32768,256]{1,0:T(8,128)} %all-gather.5.cloned.1.call-done, f32[]{:T(128)} %constant.76.clone.1), dimensions={0}, to_apply=%region_1.3 | reduce | flops 8388352 | bytes 33555460 | tf_op jit(solution)/shard_map/reduce_sum | solution.py:60
  325.1 5.8 cholesky.44
  331.0 0.6 compare_reduce_fusion.1
  331.6 0.7 fusion.21
  332.3 4.9 custom-call.11
  338.6 0.7 gather_fusion.4
  339.3 0.7 gather_fusion.3
  340.1 0.7 gather_fusion.5
  341.1 0.7 copy.153
  341.8 232.0 %all-gather.7.cloned.1.call-done = f32[32768,256]{1,0:T(8,128)} async-done(((f32[64,256]{1,0:T(8,128)}), f32[32768,256]{1,0:T(8,128)}) %all-gather.7.cloned.1.call-update) | async-done | bytes 33554448 | tf_op jit(solution)/shard_map/all_gather | solution.py:111
  573.8 12.9 %reduce_sum.57 = f32[64,256]{1,0:T(8,128)S(1)} reduce(f32[512,64,256]{2,1,0:T(8,128)} %bitcast.138, f32[]{:T(128)} %constant.76.clone.1), dimensions={0}, to_apply=%region_5.10 | reduce | flops 8372224 | bytes 33619972 | tf_op jit(solution)/shard_map/reduce_sum | solution.py:111
  586.8 15.0 %reduce_sum.58 = f32[256]{0:T(256)S(1)} reduce(f32[32768,256]{1,0:T(8,128)} %all-gather.7.cloned.1.call-done, f32[]{:T(128)} %constant.76.clone.1), dimensions={0}, to_apply=%region_6.11 | reduce | flops 8388352 | bytes 33555460 | tf_op jit(solution)/shard_map/reduce_sum | solution.py:60
  602.1 5.8 cholesky.55
  608.0 0.6 compare_reduce_fusion
  608.6 0.7 fusion.22
  609.3 4.9 custom-call.13
  616.1 10.2 %all_to_all.36 = f32[8,1,6144]{2,1,0:T(1,128)S(1)} all-to-all(f32[8,1,6144]{2,1,0:T(1,128)S(1)} %reshape.208), channel_id=1, replica_groups=mesh['slab'=64,'mem'=8] {'mem'}, dimensions={0} | all-to-all | bytes 393216 | tf_op jit(solution)/shard_map/all_to_all | solution.py:114
  626.2 1.0 reduce.21
  627.8 0.9 all_to_all.33
  (63 shorter events, 6.9 us)
Async XLA Ops:
  7.4 14.8 %collective-permute-start = (f32[8,4,1,512]{3,0,2,1:T(8,128)S(1)}, f32[8,4,1,512]{3,0,2,1:T(8,128)S(1)}, u32[]{:S(2)}, u32[]{:S(2)}) collective-permute-start(f32[8,4,1,512]{3,0,2,1:T(8,128)S(1)} %copy.138), channel_id=1, source_target_pairs={{8,0},{16,8},{24,16},{32,24},{40,32},{48,40},{56,48},{64,56},{72,6... | collective-permute-start | bytes 196616 | tf_op jit(solution)/shard_map/ppermute | solution.py:16
  8.7 13.5 %collective-permute-start.1 = (f32[8,4,1,512]{3,0,2,1:T(8,128)S(1)}, f32[8,4,1,512]{3,0,2,1:T(8,128)S(1)}, u32[]{:S(2)}, u32[]{:S(2)}) collective-permute-start(f32[8,4,1,512]{3,0,2,1:T(8,128)S(1)} %copy.138), channel_id=1, source_target_pairs={{0,8},{8,16},{16,24},{24,32},{32,40},{40,48},{48,56},{56,64},{64,7... | collective-permute-start | bytes 196616 | tf_op jit(solution)/shard_map/ppermute | solution.py:15
  31.6 15.9 %all-to-all-start = ((f32[8,1,6144]{2,1,0:T(1,128)}), f32[8,1,6144]{2,1,0:T(1,128)S(1)}, u32[]{:S(2)}, u32[]{:S(2)}) async-start(f32[8,1,6144]{2,1,0:T(1,128)} %reshape.206), calls=%async_computation | async-start | bytes 393216 | tf_op jit(solution)/shard_map/all_to_all | solution.py:105
  41.6 255.2 %all-gather.5.cloned.1.call-start = ((), (), s32[]{:S(2)}) async-start(), calls=%async_computation.2 | async-start | bytes 33619968 | tf_op jit(solution)/shard_map/all_gather | solution.py:111
  54.3 6.6 %copy-start = (f32[2,256]{1,0:T(2,128)S(1)}, f32[2,256]{1,0:T(2,128)}, u32[]{:S(2)}) copy-start(f32[2,256]{1,0:T(2,128)} %param.21) | copy-start | bytes 6148
  58.5 515.4 %all-gather.7.cloned.1.call-start = ((), (), s32[]{:S(2)}) async-start(), calls=%async_computation.3 | async-start | bytes 33619968 | tf_op jit(solution)/shard_map/all_gather | solution.py:111
  309.7 27.5 %copy-start.4 = (f32[2,64,256]{2,1,0:T(8,128)S(1)}, f32[2,64,256]{2,1,0:T(8,128)}, u32[]{:S(2)}) copy-start(f32[2,64,256]{2,1,0:T(8,128)} %param.23) | copy-start | bytes 393220
  324.8 16.0 %copy-start.1 = (pred[256]{0:T(512)(128)(4,1)S(1)}, pred[256]{0:T(512)(128)(4,1)}, u32[]{:S(2)}) copy-start(pred[256]{0:T(512)(128)(4,1)} %get-tuple-element.6) | copy-start | bytes 772
  324.8 16.0 %copy-start.2 = (pred[256]{0:T(512)(128)(4,1)S(1)}, pred[256]{0:T(512)(128)(4,1)}, u32[]{:S(2)}) copy-start(pred[256]{0:T(512)(128)(4,1)} %get-tuple-element.8) | copy-start | bytes 772
  324.8 16.0 %copy-start.3 = (pred[256]{0:T(512)(128)(4,1)S(1)}, pred[256]{0:T(512)(128)(4,1)}, u32[]{:S(2)}) copy-start(pred[256]{0:T(512)(128)(4,1)} %get-tuple-element.10) | copy-start | bytes 772
Sparse Core Ops, SparseCore 0:
  58.6 238.1 all-gather.4
  341.9 231.8 all-gather.6
